TPU v7x, 512 devices: a whole 4x8x8 slice. The times are simulated.
512 devices in a mesh: pipe: 8 (over z), expert: 32 (over y, x), dp: 2 (over core).
Axes of the slice: x: 4, y: 8, z: 8, core: 2. Of those that a mesh axis runs over, the one named last changes fastest.
Arguments:
- saved: bfloat16 [1, 8, 8192, 2560], P(None, 'pipe', ('expert', 'dp')), may hold values from -6 to 6
- cotangent: bfloat16 [8192, 2560], P(('expert', 'dp'), 'pipe'), may hold values from -1.1953125 to 1.1953125
- routes: int32 [1, 8, 8192, 1], P(None, 'pipe', ('expert', 'dp')), may hold values from 0 to 7; in each aligned block of 16 rows (0 to 15, 16 to 31, ..., all dimensions but the last counted through in order) at most 2 rows name the same one
- w_gate: bfloat16 [1, 8, 8192, 2560], P(None, 'pipe', 'expert', 'dp'), may hold values from -0.125 to 0.125
- w_up: bfloat16 [1, 8, 8192, 2560], P(None, 'pipe', 'expert', 'dp'), may hold values from -0.125 to 0.125
- w_down: bfloat16 [1, 8, 8192, 2560], P(None, 'pipe', 'expert', 'dp'), may hold values from -0.0625 to 0.0625
Outputs:
- grad_gate: bfloat16 [1, 8, 8192, 2560], P(None, 'pipe', 'expert', 'dp')
- grad_up: bfloat16 [1, 8, 8192, 2560], P(None, 'pipe', 'expert', 'dp')
Inputs may be any that keep to these rules, and one draw needn't show every extreme that they name: In each aligned block of 16 rows of routes (one micro-batch of one device, rows taken in order over all leading dimensions) no expert is named more than 2 times.
All inputs are finite; a program needn't handle non-finite values.
Results may differ from a plain program's by a relative error of at most 0.017.
Values may be sent and summed in bfloat16 or wider, within the bound.
No kernel may reach another device: no remote copies, remote signals or barrier semaphores. Data moves between devices by JAX's collectives and lax.ppermute only.
A program may use at most 64 MiB of HBM per device.

v0:
```python
import jax
import jax.numpy as jnp
from jax import lax
from jax.sharding import PartitionSpec as P

GROUP = 4
MICRO = 8
epsilon = 1e-06


def shifted(block, axis, distance):
    devices = range(lax.axis_size(axis))
    route = [(i - distance, i) for i in devices if i - distance in devices]
    return lax.ppermute(block, axis, route)


def slot_tables(route_ids, experts, capacity):
    onehot = (route_ids[..., None] == jnp.arange(experts, dtype=jnp.int32)).astype(jnp.int32)
    ranking = jnp.sum((jnp.cumsum(onehot, axis=2) - onehot) * onehot, axis=3)
    slot_ids = route_ids * capacity + ranking
    positions = jnp.arange(experts * capacity, dtype=jnp.int32)[:, None]
    placing = (slot_ids[..., None, :] == positions).astype(jnp.bfloat16)
    return (placing, slot_ids)


def shards(saved, cotangent, routes, w_gate, w_up, w_down):
    sections = lax.axis_size("pipe")
    width_all = lax.axis_size("expert")
    section_index = lax.axis_index("pipe")
    stretches = saved.shape[0]
    tok_dev = saved.shape[2]
    tok_mb = tok_dev // MICRO
    experts = width_all // GROUP
    capacity = max(2, tok_mb // experts)
    period = sections + MICRO - 1
    slot_count = width_all * capacity
    head_grad = lax.all_gather(cotangent, "pipe", axis=1, tiled=True)
    feature_count = head_grad.shape[1]
    slabs = (
        lax.all_gather(w_gate, "dp", axis=3, tiled=True),
        lax.all_gather(w_up, "dp", axis=3, tiled=True),
        lax.all_gather(w_down, "dp", axis=3, tiled=True),
    )
    gate_w = slabs[0][:, 0]
    up_w = slabs[1][:, 0]
    down_w = slabs[2][:, 0]
    hidden = gate_w.shape[1]
    inputs_f = saved[:, 0].astype(jnp.float32).reshape(stretches, MICRO, tok_mb, feature_count)
    norm_scale = lax.rsqrt(jnp.mean(inputs_f * inputs_f, axis=3, keepdims=True) + epsilon)
    unit_f = inputs_f * norm_scale
    unit_b = unit_f.astype(jnp.bfloat16)
    route_ids = routes[:, 0, :, 0].reshape(stretches, MICRO, tok_mb)
    placing, slot_ids = slot_tables(route_ids, experts, capacity)
    unit_slots = jnp.einsum("vmst,vmtd->vmsd", placing, unit_b, preferred_element_type=jnp.float32)
    unit_slots = unit_slots.astype(jnp.bfloat16).reshape(
        stretches, MICRO, experts, capacity, feature_count
    )
    unit_send = jnp.repeat(unit_slots, GROUP, axis=2)
    unit_recv = lax.all_to_all(unit_send, "expert", split_axis=2, concat_axis=2, tiled=True)
    unit_rows = unit_recv.reshape(stretches, MICRO, slot_count, feature_count)
    top_section = section_index == sections - 1

    def tick_step(tick_index, loop_state):
        carried, gate_store, up_store = loop_state
        stretch_index = 0
        micro_raw = tick_index - (sections - 1 - section_index)
        active = (micro_raw >= 0) & (micro_raw < MICRO)
        micro_index = jnp.clip(micro_raw, 0, MICRO - 1)
        seed_rows = lax.dynamic_slice_in_dim(head_grad, micro_index * tok_mb, tok_mb, 0)
        grad_in = jnp.where(top_section, seed_rows, carried)
        grad_in = jnp.where(active, grad_in, jnp.zeros_like(grad_in))
        place_now = placing[stretch_index, micro_index].reshape(experts, capacity, tok_mb)
        slot_grads = jnp.einsum(
            "ect,td->ecd", place_now, grad_in, preferred_element_type=jnp.float32
        )
        sending = jnp.repeat(slot_grads.astype(jnp.bfloat16), GROUP, axis=0)
        grad_rows = lax.all_to_all(
            sending, "expert", split_axis=0, concat_axis=0, tiled=True
        ).reshape(slot_count, feature_count)
        gate_slab = gate_w[stretch_index]
        up_slab = up_w[stretch_index]
        down_slab = down_w[stretch_index]
        unit_now = unit_rows[stretch_index, micro_index]
        gate = jnp.einsum("rd,hd->rh", unit_now, gate_slab, preferred_element_type=jnp.float32)
        up = jnp.einsum("rd,hd->rh", unit_now, up_slab, preferred_element_type=jnp.float32)
        hidden_grad = jnp.einsum(
            "rd,hd->rh", grad_rows, down_slab, preferred_element_type=jnp.float32
        )
        sigmoid_gate = jax.nn.sigmoid(gate)
        gate_grad = (hidden_grad * up * sigmoid_gate * (1.0 + gate * (1.0 - sigmoid_gate))).astype(
            jnp.bfloat16
        )
        up_grad = (hidden_grad * gate * sigmoid_gate).astype(jnp.bfloat16)
        partial_value = jnp.dot(gate_grad, gate_slab, preferred_element_type=jnp.float32)
        partial_value = (
            partial_value + jnp.dot(up_grad, up_slab, preferred_element_type=jnp.float32)
        ).astype(jnp.bfloat16)
        returned = lax.all_to_all(
            partial_value.reshape(width_all, capacity, feature_count),
            "expert",
            split_axis=0,
            concat_axis=0,
            tiled=True,
        )
        summed = (
            returned.reshape(experts, GROUP, capacity, feature_count)
            .astype(jnp.float32)
            .sum(axis=1)
        )
        unit_grad = jnp.take(
            summed.reshape(experts * capacity, feature_count),
            slot_ids[stretch_index, micro_index],
            axis=0,
        )
        unit_here = unit_f[stretch_index, micro_index]
        scale_rows = norm_scale[stretch_index, micro_index]
        norm_grad = scale_rows * (
            unit_grad - unit_here * jnp.mean(unit_grad * unit_here, axis=1, keepdims=True)
        )
        grad_out = (grad_in.astype(jnp.float32) + norm_grad).astype(jnp.bfloat16)
        carried = shifted(grad_out, "pipe", -1)
        gate_store = jnp.where(
            active, gate_store.at[stretch_index, micro_index].set(gate_grad), gate_store
        )
        up_store = jnp.where(active, up_store.at[stretch_index, micro_index].set(up_grad), up_store)
        return (carried, gate_store, up_store)

    start_state = (
        jnp.zeros((tok_mb, feature_count), jnp.bfloat16),
        jnp.zeros((stretches, MICRO, slot_count, hidden), jnp.bfloat16),
        jnp.zeros((stretches, MICRO, slot_count, hidden), jnp.bfloat16),
    )
    final_state = lax.fori_loop(0, period, tick_step, start_state)
    flat_units = unit_rows.reshape(stretches, MICRO * slot_count, feature_count)
    part_gate = jnp.einsum(
        "vrh,vrd->vhd",
        final_state[1].reshape(stretches, MICRO * slot_count, hidden),
        flat_units,
        preferred_element_type=jnp.float32,
    )
    part_up = jnp.einsum(
        "vrh,vrd->vhd",
        final_state[2].reshape(stretches, MICRO * slot_count, hidden),
        flat_units,
        preferred_element_type=jnp.float32,
    )
    totals = (
        lax.psum_scatter(
            part_gate.astype(jnp.bfloat16), "dp", scatter_dimension=2, tiled=True
        ).astype(jnp.float32),
        lax.psum_scatter(
            part_up.astype(jnp.bfloat16), "dp", scatter_dimension=2, tiled=True
        ).astype(jnp.float32),
    )
    grad_gate = totals[0].astype(jnp.bfloat16)[:, None]
    grad_up = totals[1].astype(jnp.bfloat16)[:, None]
    return (grad_gate, grad_up)


def solution(mesh):
    in_specs = (
        P(None, "pipe", ("expert", "dp"), None),
        P(("expert", "dp"), "pipe"),
        P(None, "pipe", ("expert", "dp"), None),
        P(None, "pipe", "expert", "dp"),
        P(None, "pipe", "expert", "dp"),
        P(None, "pipe", "expert", "dp"),
    )
    out_specs = (P(None, "pipe", "expert", "dp"), P(None, "pipe", "expert", "dp"))
    return jax.shard_map(shards, mesh=mesh, in_specs=in_specs, out_specs=out_specs, check_vma=False)
```

profile of v0, /device:TPU:1, one launch (start us, length us, event | category | flops | bytes accessed | tf_op | source)
XLA Modules:
  0.0 954.3 jit_solution(4917801500919075737)
XLA Ops:
  16.8 10.5 %all-to-all-start.2 = ((bf16[1,8,32,2,2560]{4,3,1,0,2:T(2,128)(2,1)}), bf16[1,8,32,2,2560]{4,3,1,0,2:T(2,128)(2,1)S(1)}, u32[]{:S(2)}, u32[]{:S(2)}) async-start(bf16[1,8,32,2,2560]{4,3,1,0,2:T(2,128)(2,1)} %bitcast.139), calls=%async_computation.2 | async-start | bytes 5242880 | tf_op jit(solution)/shard_map/all_to_all | solution.py:59
  29.6 28.2 %all_gather.12 = bf16[128,2560]{0,1:T(8,128)(2,1)S(1)} all-gather(bf16[128,320]{0,1:T(8,128)(2,1)S(1)} %copy-done.6), channel_id=1, replica_groups=mesh['pipe'=8,'expert'=32,'dp'=2] {'pipe'}, dimensions={1}, use_global_device_ids=true | all-gather | bytes 737280 | tf_op jit(solution)/shard_map/all_gather | solution.py:37
  61.6 25.4 %all-to-all-done.2 = bf16[1,8,32,2,2560]{4,3,1,0,2:T(2,128)(2,1)S(1)} async-done(((bf16[1,8,32,2,2560]{4,3,1,0,2:T(2,128)(2,1)}), bf16[1,8,32,2,2560]{4,3,1,0,2:T(2,128)(2,1)S(1)}, u32[]{:S(2)}, u32[]{:S(2)}) %all-to-all-start.2) | async-done | bytes 2621472 | tf_op jit(solution)/shard_map/all_to_all | solution.py:59
  101.3 753.9 %while.21 = (s32[]{:T(128)}, bf16[16,2560]{1,0:T(8,128)(2,1)S(1)}, bf16[1,8,64,256]{3,2,1,0:T(8,128)(2,1)}, bf16[1,8,64,256]{3,2,1,0:T(8,128)(2,1)}, s32[]{:T(12...) while((s32[]{:T(128)}, bf16[16,2560]{1,0:T(8,128)(2,1)S(1)}, ...), condition=%wide.region_7.8_spmd, body=%wide.region_3.7_spmd.sunk | while | flops 422298752 | bytes 31975776 | solution.py:133
  111.0 10.5 %all-to-all-done = bf16[32,2,2560]{2,1,0:T(2,128)(2,1)S(1)} async-done(((bf16[32,2,2560]{2,1,0:T(2,128)(2,1)}), bf16[32,2,2560]{2,1,0:T(2,128)(2,1)S(1)}, u32[]{:S(2)}, u32[]{:S(2)}) %all-to-all-start) | async-done | bytes 327712 | tf_op jit(solution)/shard_map/while/body/eval_jaxpr/all_to_all | solution.py:77
  135.3 10.7 %all-to-all-done.1 = bf16[32,2,2560]{2,1,0:T(2,128)(2,1)S(1)} async-done(((bf16[32,2,2560]{2,1,0:T(2,128)(2,1)}), bf16[32,2,2560]{2,1,0:T(2,128)(2,1)S(1)}, u32[]{:S(2)}, u32[]{:S(2)}) %all-to-all-start.1) | async-done | bytes 327712 | tf_op jit(solution)/shard_map/while/body/eval_jaxpr/all_to_all | solution.py:98
  164.0 10.1 %all-to-all-done = bf16[32,2,2560]{2,1,0:T(2,128)(2,1)S(1)} async-done(((bf16[32,2,2560]{2,1,0:T(2,128)(2,1)}), bf16[32,2,2560]{2,1,0:T(2,128)(2,1)S(1)}, u32[]{:S(2)}, u32[]{:S(2)}) %all-to-all-start) | async-done | bytes 327712 | tf_op jit(solution)/shard_map/while/body/eval_jaxpr/all_to_all | solution.py:77
  186.3 10.7 %all-to-all-done.1 = bf16[32,2,2560]{2,1,0:T(2,128)(2,1)S(1)} async-done(((bf16[32,2,2560]{2,1,0:T(2,128)(2,1)}), bf16[32,2,2560]{2,1,0:T(2,128)(2,1)S(1)}, u32[]{:S(2)}, u32[]{:S(2)}) %all-to-all-start.1) | async-done | bytes 327712 | tf_op jit(solution)/shard_map/while/body/eval_jaxpr/all_to_all | solution.py:98
  213.1 10.0 %all-to-all-done = bf16[32,2,2560]{2,1,0:T(2,128)(2,1)S(1)} async-done(((bf16[32,2,2560]{2,1,0:T(2,128)(2,1)}), bf16[32,2,2560]{2,1,0:T(2,128)(2,1)S(1)}, u32[]{:S(2)}, u32[]{:S(2)}) %all-to-all-start) | async-done | bytes 327712 | tf_op jit(solution)/shard_map/while/body/eval_jaxpr/all_to_all | solution.py:77
  234.9 10.6 %all-to-all-done.1 = bf16[32,2,2560]{2,1,0:T(2,128)(2,1)S(1)} async-done(((bf16[32,2,2560]{2,1,0:T(2,128)(2,1)}), bf16[32,2,2560]{2,1,0:T(2,128)(2,1)S(1)}, u32[]{:S(2)}, u32[]{:S(2)}) %all-to-all-start.1) | async-done | bytes 327712 | tf_op jit(solution)/shard_map/while/body/eval_jaxpr/all_to_all | solution.py:98
  261.4 10.0 %all-to-all-done = bf16[32,2,2560]{2,1,0:T(2,128)(2,1)S(1)} async-done(((bf16[32,2,2560]{2,1,0:T(2,128)(2,1)}), bf16[32,2,2560]{2,1,0:T(2,128)(2,1)S(1)}, u32[]{:S(2)}, u32[]{:S(2)}) %all-to-all-start) | async-done | bytes 327712 | tf_op jit(solution)/shard_map/while/body/eval_jaxpr/all_to_all | solution.py:77
  283.1 10.6 %all-to-all-done.1 = bf16[32,2,2560]{2,1,0:T(2,128)(2,1)S(1)} async-done(((bf16[32,2,2560]{2,1,0:T(2,128)(2,1)}), bf16[32,2,2560]{2,1,0:T(2,128)(2,1)S(1)}, u32[]{:S(2)}, u32[]{:S(2)}) %all-to-all-start.1) | async-done | bytes 327712 | tf_op jit(solution)/shard_map/while/body/eval_jaxpr/all_to_all | solution.py:98
  311.2 10.0 %all-to-all-done = bf16[32,2,2560]{2,1,0:T(2,128)(2,1)S(1)} async-done(((bf16[32,2,2560]{2,1,0:T(2,128)(2,1)}), bf16[32,2,2560]{2,1,0:T(2,128)(2,1)S(1)}, u32[]{:S(2)}, u32[]{:S(2)}) %all-to-all-start) | async-done | bytes 327712 | tf_op jit(solution)/shard_map/while/body/eval_jaxpr/all_to_all | solution.py:77
  332.9 10.6 %all-to-all-done.1 = bf16[32,2,2560]{2,1,0:T(2,128)(2,1)S(1)} async-done(((bf16[32,2,2560]{2,1,0:T(2,128)(2,1)}), bf16[32,2,2560]{2,1,0:T(2,128)(2,1)S(1)}, u32[]{:S(2)}, u32[]{:S(2)}) %all-to-all-start.1) | async-done | bytes 327712 | tf_op jit(solution)/shard_map/while/body/eval_jaxpr/all_to_all | solution.py:98
  360.3 10.0 %all-to-all-done = bf16[32,2,2560]{2,1,0:T(2,128)(2,1)S(1)} async-done(((bf16[32,2,2560]{2,1,0:T(2,128)(2,1)}), bf16[32,2,2560]{2,1,0:T(2,128)(2,1)S(1)}, u32[]{:S(2)}, u32[]{:S(2)}) %all-to-all-start) | async-done | bytes 327712 | tf_op jit(solution)/shard_map/while/body/eval_jaxpr/all_to_all | solution.py:77
  382.0 11.0 %all-to-all-done.1 = bf16[32,2,2560]{2,1,0:T(2,128)(2,1)S(1)} async-done(((bf16[32,2,2560]{2,1,0:T(2,128)(2,1)}), bf16[32,2,2560]{2,1,0:T(2,128)(2,1)S(1)}, u32[]{:S(2)}, u32[]{:S(2)}) %all-to-all-start.1) | async-done | bytes 327712 | tf_op jit(solution)/shard_map/while/body/eval_jaxpr/all_to_all | solution.py:98
  409.2 10.5 %all-to-all-done = bf16[32,2,2560]{2,1,0:T(2,128)(2,1)S(1)} async-done(((bf16[32,2,2560]{2,1,0:T(2,128)(2,1)}), bf16[32,2,2560]{2,1,0:T(2,128)(2,1)S(1)}, u32[]{:S(2)}, u32[]{:S(2)}) %all-to-all-start) | async-done | bytes 327712 | tf_op jit(solution)/shard_map/while/body/eval_jaxpr/all_to_all | solution.py:77
  431.3 12.4 %all-to-all-done.1 = bf16[32,2,2560]{2,1,0:T(2,128)(2,1)S(1)} async-done(((bf16[32,2,2560]{2,1,0:T(2,128)(2,1)}), bf16[32,2,2560]{2,1,0:T(2,128)(2,1)S(1)}, u32[]{:S(2)}, u32[]{:S(2)}) %all-to-all-start.1) | async-done | bytes 327712 | tf_op jit(solution)/shard_map/while/body/eval_jaxpr/all_to_all | solution.py:98
  460.5 10.3 %all-to-all-done = bf16[32,2,2560]{2,1,0:T(2,128)(2,1)S(1)} async-done(((bf16[32,2,2560]{2,1,0:T(2,128)(2,1)}), bf16[32,2,2560]{2,1,0:T(2,128)(2,1)S(1)}, u32[]{:S(2)}, u32[]{:S(2)}) %all-to-all-start) | async-done | bytes 327712 | tf_op jit(solution)/shard_map/while/body/eval_jaxpr/all_to_all | solution.py:77
  482.5 11.1 %all-to-all-done.1 = bf16[32,2,2560]{2,1,0:T(2,128)(2,1)S(1)} async-done(((bf16[32,2,2560]{2,1,0:T(2,128)(2,1)}), bf16[32,2,2560]{2,1,0:T(2,128)(2,1)S(1)}, u32[]{:S(2)}, u32[]{:S(2)}) %all-to-all-start.1) | async-done | bytes 327712 | tf_op jit(solution)/shard_map/while/body/eval_jaxpr/all_to_all | solution.py:98
  512.0 12.4 %all-to-all-done = bf16[32,2,2560]{2,1,0:T(2,128)(2,1)S(1)} async-done(((bf16[32,2,2560]{2,1,0:T(2,128)(2,1)}), bf16[32,2,2560]{2,1,0:T(2,128)(2,1)S(1)}, u32[]{:S(2)}, u32[]{:S(2)}) %all-to-all-start) | async-done | bytes 327712 | tf_op jit(solution)/shard_map/while/body/eval_jaxpr/all_to_all | solution.py:77
  536.1 11.1 %all-to-all-done.1 = bf16[32,2,2560]{2,1,0:T(2,128)(2,1)S(1)} async-done(((bf16[32,2,2560]{2,1,0:T(2,128)(2,1)}), bf16[32,2,2560]{2,1,0:T(2,128)(2,1)S(1)}, u32[]{:S(2)}, u32[]{:S(2)}) %all-to-all-start.1) | async-done | bytes 327712 | tf_op jit(solution)/shard_map/while/body/eval_jaxpr/all_to_all | solution.py:98
  563.9 11.3 %all-to-all-done = bf16[32,2,2560]{2,1,0:T(2,128)(2,1)S(1)} async-done(((bf16[32,2,2560]{2,1,0:T(2,128)(2,1)}), bf16[32,2,2560]{2,1,0:T(2,128)(2,1)S(1)}, u32[]{:S(2)}, u32[]{:S(2)}) %all-to-all-start) | async-done | bytes 327712 | tf_op jit(solution)/shard_map/while/body/eval_jaxpr/all_to_all | solution.py:77
  588.1 10.6 %all-to-all-done.1 = bf16[32,2,2560]{2,1,0:T(2,128)(2,1)S(1)} async-done(((bf16[32,2,2560]{2,1,0:T(2,128)(2,1)}), bf16[32,2,2560]{2,1,0:T(2,128)(2,1)S(1)}, u32[]{:S(2)}, u32[]{:S(2)}) %all-to-all-start.1) | async-done | bytes 327712 | tf_op jit(solution)/shard_map/while/body/eval_jaxpr/all_to_all | solution.py:98
  637.0 10.6 %all-to-all-done.1 = bf16[32,2,2560]{2,1,0:T(2,128)(2,1)S(1)} async-done(((bf16[32,2,2560]{2,1,0:T(2,128)(2,1)}), bf16[32,2,2560]{2,1,0:T(2,128)(2,1)S(1)}, u32[]{:S(2)}, u32[]{:S(2)}) %all-to-all-start.1) | async-done | bytes 327712 | tf_op jit(solution)/shard_map/while/body/eval_jaxpr/all_to_all | solution.py:98
  686.3 10.6 %all-to-all-done.1 = bf16[32,2,2560]{2,1,0:T(2,128)(2,1)S(1)} async-done(((bf16[32,2,2560]{2,1,0:T(2,128)(2,1)}), bf16[32,2,2560]{2,1,0:T(2,128)(2,1)S(1)}, u32[]{:S(2)}, u32[]{:S(2)}) %all-to-all-start.1) | async-done | bytes 327712 | tf_op jit(solution)/shard_map/while/body/eval_jaxpr/all_to_all | solution.py:98
  735.1 10.6 %all-to-all-done.1 = bf16[32,2,2560]{2,1,0:T(2,128)(2,1)S(1)} async-done(((bf16[32,2,2560]{2,1,0:T(2,128)(2,1)}), bf16[32,2,2560]{2,1,0:T(2,128)(2,1)S(1)}, u32[]{:S(2)}, u32[]{:S(2)}) %all-to-all-start.1) | async-done | bytes 327712 | tf_op jit(solution)/shard_map/while/body/eval_jaxpr/all_to_all | solution.py:98
  784.1 10.6 %all-to-all-done.1 = bf16[32,2,2560]{2,1,0:T(2,128)(2,1)S(1)} async-done(((bf16[32,2,2560]{2,1,0:T(2,128)(2,1)}), bf16[32,2,2560]{2,1,0:T(2,128)(2,1)S(1)}, u32[]{:S(2)}, u32[]{:S(2)}) %all-to-all-start.1) | async-done | bytes 327712 | tf_op jit(solution)/shard_map/while/body/eval_jaxpr/all_to_all | solution.py:98
  811.0 10.3 %all-to-all-done = bf16[32,2,2560]{2,1,0:T(2,128)(2,1)S(1)} async-done(((bf16[32,2,2560]{2,1,0:T(2,128)(2,1)}), bf16[32,2,2560]{2,1,0:T(2,128)(2,1)S(1)}, u32[]{:S(2)}, u32[]{:S(2)}) %all-to-all-start) | async-done | bytes 327712 | tf_op jit(solution)/shard_map/while/body/eval_jaxpr/all_to_all | solution.py:77
  833.0 11.8 %all-to-all-done.1 = bf16[32,2,2560]{2,1,0:T(2,128)(2,1)S(1)} async-done(((bf16[32,2,2560]{2,1,0:T(2,128)(2,1)}), bf16[32,2,2560]{2,1,0:T(2,128)(2,1)S(1)}, u32[]{:S(2)}, u32[]{:S(2)}) %all-to-all-start.1) | async-done | bytes 327712 | tf_op jit(solution)/shard_map/while/body/eval_jaxpr/all_to_all | solution.py:98
  862.0 64.3 %reduce-scatter.5.cloned.1.call-done = bf16[1,256,1280]{2,1,0:T(8,128)(2,1)} async-done(((bf16[1,256,2560]{2,1,0:T(8,128)(2,1)}), bf16[1,256,1280]{2,1,0:T(8,128)(2,1)}) %reduce-scatter.5.cloned.1.call-update) | async-done | bytes 655376 | tf_op jit(solution)/shard_map/reduce_scatter | solution.py:151
  926.3 21.4 %reduce-scatter.3.cloned.1.call-done = bf16[1,256,1280]{2,1,0:T(8,128)(2,1)} async-done(((bf16[1,256,2560]{2,1,0:T(8,128)(2,1)}), bf16[1,256,1280]{2,1,0:T(8,128)(2,1)}) %reduce-scatter.3.cloned.1.call-update) | async-done | bytes 655376 | tf_op jit(solution)/shard_map/reduce_scatter | solution.py:148
  (539 shorter events, 509.1 us)
Async XLA Ops:
  16.8 70.2 %all-to-all-start.2 = ((bf16[1,8,32,2,2560]{4,3,1,0,2:T(2,128)(2,1)}), bf16[1,8,32,2,2560]{4,3,1,0,2:T(2,128)(2,1)S(1)}, u32[]{:S(2)}, u32[]{:S(2)}) async-start(bf16[1,8,32,2,2560]{4,3,1,0,2:T(2,128)(2,1)} %bitcast.139), calls=%async_computation.2 | async-start | bytes 5242880 | tf_op jit(solution)/shard_map/all_to_all | solution.py:59
  27.3 72.5 %all-gather.4.cloned.1.call-start = ((), (), s32[]{:S(2)}) async-start(), calls=%async_computation.5 | async-start | bytes 1966080 | tf_op jit(solution)/shard_map/all_gather | solution.py:42
  28.0 71.8 %all-gather.6.cloned.1.call-start = ((), (), s32[]{:S(2)}) async-start(), calls=%async_computation.6 | async-start | bytes 1966080 | tf_op jit(solution)/shard_map/all_gather | solution.py:41
  28.8 71.1 %all-gather.8.cloned.1.call-start = ((), (), s32[]{:S(2)}) async-start(), calls=%async_computation.7 | async-start | bytes 1966080 | tf_op jit(solution)/shard_map/all_gather | solution.py:40
  29.5 896.8 %reduce-scatter.5.cloned.1.call-start = ((), (), s32[]{:S(2)}) async-start(), calls=%async_computation.9 | async-start | bytes 1966080 | tf_op jit(solution)/shard_map/reduce_scatter | solution.py:151
  103.4 18.2 %all-to-all-start = ((bf16[32,2,2560]{2,1,0:T(2,128)(2,1)}), bf16[32,2,2560]{2,1,0:T(2,128)(2,1)S(1)}, u32[]{:S(2)}, u32[]{:S(2)}) async-start(bf16[32,2,2560]{2,1,0:T(2,128)(2,1)} %bitcast.136), calls=%async_computation | async-start | bytes 655360 | tf_op jit(solution)/shard_map/while/body/eval_jaxpr/all_to_all | solution.py:77
  129.3 16.7 %all-to-all-start.1 = ((bf16[32,2,2560]{2,1,0:T(2,128)(2,1)}), bf16[32,2,2560]{2,1,0:T(2,128)(2,1)S(1)}, u32[]{:S(2)}, u32[]{:S(2)}) async-start(bf16[32,2,2560]{2,1,0:T(2,128)(2,1)} %reshape.458), calls=%async_computation.1 | async-start | bytes 655360 | tf_op jit(solution)/shard_map/while/body/eval_jaxpr/all_to_all | solution.py:98
  157.1 17.1 %all-to-all-start = ((bf16[32,2,2560]{2,1,0:T(2,128)(2,1)}), bf16[32,2,2560]{2,1,0:T(2,128)(2,1)S(1)}, u32[]{:S(2)}, u32[]{:S(2)}) async-start(bf16[32,2,2560]{2,1,0:T(2,128)(2,1)} %bitcast.136), calls=%async_computation | async-start | bytes 655360 | tf_op jit(solution)/shard_map/while/body/eval_jaxpr/all_to_all | solution.py:77
  181.9 15.0 %all-to-all-start.1 = ((bf16[32,2,2560]{2,1,0:T(2,128)(2,1)}), bf16[32,2,2560]{2,1,0:T(2,128)(2,1)S(1)}, u32[]{:S(2)}, u32[]{:S(2)}) async-start(bf16[32,2,2560]{2,1,0:T(2,128)(2,1)} %reshape.458), calls=%async_computation.1 | async-start | bytes 655360 | tf_op jit(solution)/shard_map/while/body/eval_jaxpr/all_to_all | solution.py:98
  208.2 14.9 %all-to-all-start = ((bf16[32,2,2560]{2,1,0:T(2,128)(2,1)}), bf16[32,2,2560]{2,1,0:T(2,128)(2,1)S(1)}, u32[]{:S(2)}, u32[]{:S(2)}) async-start(bf16[32,2,2560]{2,1,0:T(2,128)(2,1)} %bitcast.136), calls=%async_computation | async-start | bytes 655360 | tf_op jit(solution)/shard_map/while/body/eval_jaxpr/all_to_all | solution.py:77
  230.8 14.7 %all-to-all-start.1 = ((bf16[32,2,2560]{2,1,0:T(2,128)(2,1)}), bf16[32,2,2560]{2,1,0:T(2,128)(2,1)S(1)}, u32[]{:S(2)}, u32[]{:S(2)}) async-start(bf16[32,2,2560]{2,1,0:T(2,128)(2,1)} %reshape.458), calls=%async_computation.1 | async-start | bytes 655360 | tf_op jit(solution)/shard_map/while/body/eval_jaxpr/all_to_all | solution.py:98
  256.7 14.7 %all-to-all-start = ((bf16[32,2,2560]{2,1,0:T(2,128)(2,1)}), bf16[32,2,2560]{2,1,0:T(2,128)(2,1)S(1)}, u32[]{:S(2)}, u32[]{:S(2)}) async-start(bf16[32,2,2560]{2,1,0:T(2,128)(2,1)} %bitcast.136), calls=%async_computation | async-start | bytes 655360 | tf_op jit(solution)/shard_map/while/body/eval_jaxpr/all_to_all | solution.py:77
  306.5 14.7 %all-to-all-start = ((bf16[32,2,2560]{2,1,0:T(2,128)(2,1)}), bf16[32,2,2560]{2,1,0:T(2,128)(2,1)S(1)}, u32[]{:S(2)}, u32[]{:S(2)}) async-start(bf16[32,2,2560]{2,1,0:T(2,128)(2,1)} %bitcast.136), calls=%async_computation | async-start | bytes 655360 | tf_op jit(solution)/shard_map/while/body/eval_jaxpr/all_to_all | solution.py:77
  355.6 14.7 %all-to-all-start = ((bf16[32,2,2560]{2,1,0:T(2,128)(2,1)}), bf16[32,2,2560]{2,1,0:T(2,128)(2,1)S(1)}, u32[]{:S(2)}, u32[]{:S(2)}) async-start(bf16[32,2,2560]{2,1,0:T(2,128)(2,1)} %bitcast.136), calls=%async_computation | async-start | bytes 655360 | tf_op jit(solution)/shard_map/while/body/eval_jaxpr/all_to_all | solution.py:77
  378.0 15.0 %all-to-all-start.1 = ((bf16[32,2,2560]{2,1,0:T(2,128)(2,1)}), bf16[32,2,2560]{2,1,0:T(2,128)(2,1)S(1)}, u32[]{:S(2)}, u32[]{:S(2)}) async-start(bf16[32,2,2560]{2,1,0:T(2,128)(2,1)} %reshape.458), calls=%async_computation.1 | async-start | bytes 655360 | tf_op jit(solution)/shard_map/while/body/eval_jaxpr/all_to_all | solution.py:98
  404.6 15.1 %all-to-all-start = ((bf16[32,2,2560]{2,1,0:T(2,128)(2,1)}), bf16[32,2,2560]{2,1,0:T(2,128)(2,1)S(1)}, u32[]{:S(2)}, u32[]{:S(2)}) async-start(bf16[32,2,2560]{2,1,0:T(2,128)(2,1)} %bitcast.136), calls=%async_computation | async-start | bytes 655360 | tf_op jit(solution)/shard_map/while/body/eval_jaxpr/all_to_all | solution.py:77
  427.4 16.3 %all-to-all-start.1 = ((bf16[32,2,2560]{2,1,0:T(2,128)(2,1)}), bf16[32,2,2560]{2,1,0:T(2,128)(2,1)S(1)}, u32[]{:S(2)}, u32[]{:S(2)}) async-start(bf16[32,2,2560]{2,1,0:T(2,128)(2,1)} %reshape.458), calls=%async_computation.1 | async-start | bytes 655360 | tf_op jit(solution)/shard_map/while/body/eval_jaxpr/all_to_all | solution.py:98
  455.9 14.9 %all-to-all-start = ((bf16[32,2,2560]{2,1,0:T(2,128)(2,1)}), bf16[32,2,2560]{2,1,0:T(2,128)(2,1)S(1)}, u32[]{:S(2)}, u32[]{:S(2)}) async-start(bf16[32,2,2560]{2,1,0:T(2,128)(2,1)} %bitcast.136), calls=%async_computation | async-start | bytes 655360 | tf_op jit(solution)/shard_map/while/body/eval_jaxpr/all_to_all | solution.py:77
  478.5 15.1 %all-to-all-start.1 = ((bf16[32,2,2560]{2,1,0:T(2,128)(2,1)}), bf16[32,2,2560]{2,1,0:T(2,128)(2,1)S(1)}, u32[]{:S(2)}, u32[]{:S(2)}) async-start(bf16[32,2,2560]{2,1,0:T(2,128)(2,1)} %reshape.458), calls=%async_computation.1 | async-start | bytes 655360 | tf_op jit(solution)/shard_map/while/body/eval_jaxpr/all_to_all | solution.py:98
  505.6 18.9 %all-to-all-start = ((bf16[32,2,2560]{2,1,0:T(2,128)(2,1)}), bf16[32,2,2560]{2,1,0:T(2,128)(2,1)S(1)}, u32[]{:S(2)}, u32[]{:S(2)}) async-start(bf16[32,2,2560]{2,1,0:T(2,128)(2,1)} %bitcast.136), calls=%async_computation | async-start | bytes 655360 | tf_op jit(solution)/shard_map/while/body/eval_jaxpr/all_to_all | solution.py:77
  532.2 15.1 %all-to-all-start.1 = ((bf16[32,2,2560]{2,1,0:T(2,128)(2,1)}), bf16[32,2,2560]{2,1,0:T(2,128)(2,1)S(1)}, u32[]{:S(2)}, u32[]{:S(2)}) async-start(bf16[32,2,2560]{2,1,0:T(2,128)(2,1)} %reshape.458), calls=%async_computation.1 | async-start | bytes 655360 | tf_op jit(solution)/shard_map/while/body/eval_jaxpr/all_to_all | solution.py:98
  559.3 15.9 %all-to-all-start = ((bf16[32,2,2560]{2,1,0:T(2,128)(2,1)}), bf16[32,2,2560]{2,1,0:T(2,128)(2,1)S(1)}, u32[]{:S(2)}, u32[]{:S(2)}) async-start(bf16[32,2,2560]{2,1,0:T(2,128)(2,1)} %bitcast.136), calls=%async_computation | async-start | bytes 655360 | tf_op jit(solution)/shard_map/while/body/eval_jaxpr/all_to_all | solution.py:77
  582.9 15.9 %all-to-all-start.1 = ((bf16[32,2,2560]{2,1,0:T(2,128)(2,1)}), bf16[32,2,2560]{2,1,0:T(2,128)(2,1)S(1)}, u32[]{:S(2)}, u32[]{:S(2)}) async-start(bf16[32,2,2560]{2,1,0:T(2,128)(2,1)} %reshape.458), calls=%async_computation.1 | async-start | bytes 655360 | tf_op jit(solution)/shard_map/while/body/eval_jaxpr/all_to_all | solution.py:98
  610.6 14.7 %all-to-all-start = ((bf16[32,2,2560]{2,1,0:T(2,128)(2,1)}), bf16[32,2,2560]{2,1,0:T(2,128)(2,1)S(1)}, u32[]{:S(2)}, u32[]{:S(2)}) async-start(bf16[32,2,2560]{2,1,0:T(2,128)(2,1)} %bitcast.136), calls=%async_computation | async-start | bytes 655360 | tf_op jit(solution)/shard_map/while/body/eval_jaxpr/all_to_all | solution.py:77
  632.9 14.7 %all-to-all-start.1 = ((bf16[32,2,2560]{2,1,0:T(2,128)(2,1)}), bf16[32,2,2560]{2,1,0:T(2,128)(2,1)S(1)}, u32[]{:S(2)}, u32[]{:S(2)}) async-start(bf16[32,2,2560]{2,1,0:T(2,128)(2,1)} %reshape.458), calls=%async_computation.1 | async-start | bytes 655360 | tf_op jit(solution)/shard_map/while/body/eval_jaxpr/all_to_all | solution.py:98
  659.9 14.7 %all-to-all-start = ((bf16[32,2,2560]{2,1,0:T(2,128)(2,1)}), bf16[32,2,2560]{2,1,0:T(2,128)(2,1)S(1)}, u32[]{:S(2)}, u32[]{:S(2)}) async-start(bf16[32,2,2560]{2,1,0:T(2,128)(2,1)} %bitcast.136), calls=%async_computation | async-start | bytes 655360 | tf_op jit(solution)/shard_map/while/body/eval_jaxpr/all_to_all | solution.py:77
  708.7 14.7 %all-to-all-start = ((bf16[32,2,2560]{2,1,0:T(2,128)(2,1)}), bf16[32,2,2560]{2,1,0:T(2,128)(2,1)S(1)}, u32[]{:S(2)}, u32[]{:S(2)}) async-start(bf16[32,2,2560]{2,1,0:T(2,128)(2,1)} %bitcast.136), calls=%async_computation | async-start | bytes 655360 | tf_op jit(solution)/shard_map/while/body/eval_jaxpr/all_to_all | solution.py:77
  731.1 14.7 %all-to-all-start.1 = ((bf16[32,2,2560]{2,1,0:T(2,128)(2,1)}), bf16[32,2,2560]{2,1,0:T(2,128)(2,1)S(1)}, u32[]{:S(2)}, u32[]{:S(2)}) async-start(bf16[32,2,2560]{2,1,0:T(2,128)(2,1)} %reshape.458), calls=%async_computation.1 | async-start | bytes 655360 | tf_op jit(solution)/shard_map/while/body/eval_jaxpr/all_to_all | solution.py:98
  757.6 14.7 %all-to-all-start = ((bf16[32,2,2560]{2,1,0:T(2,128)(2,1)}), bf16[32,2,2560]{2,1,0:T(2,128)(2,1)S(1)}, u32[]{:S(2)}, u32[]{:S(2)}) async-start(bf16[32,2,2560]{2,1,0:T(2,128)(2,1)} %bitcast.136), calls=%async_computation | async-start | bytes 655360 | tf_op jit(solution)/shard_map/while/body/eval_jaxpr/all_to_all | solution.py:77
  806.4 14.9 %all-to-all-start = ((bf16[32,2,2560]{2,1,0:T(2,128)(2,1)}), bf16[32,2,2560]{2,1,0:T(2,128)(2,1)S(1)}, u32[]{:S(2)}, u32[]{:S(2)}) async-start(bf16[32,2,2560]{2,1,0:T(2,128)(2,1)} %bitcast.136), calls=%async_computation | async-start | bytes 655360 | tf_op jit(solution)/shard_map/while/body/eval_jaxpr/all_to_all | solution.py:77
  829.0 15.8 %all-to-all-start.1 = ((bf16[32,2,2560]{2,1,0:T(2,128)(2,1)}), bf16[32,2,2560]{2,1,0:T(2,128)(2,1)S(1)}, u32[]{:S(2)}, u32[]{:S(2)}) async-start(bf16[32,2,2560]{2,1,0:T(2,128)(2,1)} %reshape.458), calls=%async_computation.1 | async-start | bytes 655360 | tf_op jit(solution)/shard_map/while/body/eval_jaxpr/all_to_all | solution.py:98
  859.1 88.6 %reduce-scatter.3.cloned.1.call-start = ((), (), s32[]{:S(2)}) async-start(), calls=%async_computation.8 | async-start | bytes 1966080 | tf_op jit(solution)/shard_map/reduce_scatter | solution.py:148
  (70 other events, 661.9 us)
Sparse Core Ops, SparseCore 0:
  30.2 23.7 all-gather.3
  56.1 18.8 all-gather.5
  77.0 18.8 all-gather.7
  859.2 67.0 reduce-scatter.4
  929.5 18.1 reduce-scatter.2
where the time goes:
time: 959 us; the launch traced here: 954 us
  waiting for transfers between devices  511 us (53%)
  starting transfers between devices  159 us (17%)
  matrix products  123 us (13%)
  local copies, waits for them, and re-layouts  62.3 us (6%)
  other arithmetic  55 us (6%)
  blocking collectives  28.2 us (3%)
  between operations  13.9 us (1%)
    all_to_all x15, waiting for transfers between devices, tick_step(): lax.all_to_all(partial_value.reshape(width_all, capacity, feature_count),...  164 us
    all_to_all x15, waiting for transfers between devices, tick_step(): lax.all_to_all(sending, 'expert', split_axis=0, concat_axis=0, tiled=True)  156 us
    ppermute x15, waiting for transfers between devices, shifted(): return lax.ppermute(block, axis, route)  77.9 us
    all_to_all x15, starting transfers between devices, tick_step(): lax.all_to_all(sending, 'expert', split_axis=0, concat_axis=0, tiled=True)  66.2 us
    reduce_scatter x1, waiting for transfers between devices, shards(): lax.psum_scatter(part_up.astype(jnp.bfloat16), 'dp', scatter_dimension=2,...  64.3 us
    all_to_all x15, starting transfers between devices, tick_step(): lax.all_to_all(partial_value.reshape(width_all, capacity, feature_count),...  62.6 us
    dot_general x15, matrix products, tick_step(): jnp.einsum('rd,hd->rh', unit_now, gate_slab, preferred_element_type=jnp.f...  41.8 us
    dot_general x15, matrix products, tick_step(): jnp.einsum('rd,hd->rh', unit_now, up_slab, preferred_element_type=jnp.flo...  40 us
  transfers between devices with their start and end apart: 51, of which 48 were waited for; matrix products, arithmetic and copies ran while one was open for 3% of the time, Pallas kernels for 0%

commit v1 on v0

--- a/solution.py
+++ b/solution.py
@@ -6,6 +6,13 @@
 GROUP = 4
 MICRO = 8
 epsilon = 1e-06
+
+
+def stacked_exchange(shard, name, split, join):
+    size = lax.axis_size(name)
+    blocks = jnp.stack(jnp.split(shard, size, axis=split), axis=0)
+    blocks = lax.all_to_all(blocks, name, split_axis=0, concat_axis=0)
+    return jnp.concatenate(blocks, axis=join)
 
 
 def shifted(block, axis, distance):
@@ -56,7 +63,7 @@
         stretches, MICRO, experts, capacity, feature_count
     )
     unit_send = jnp.repeat(unit_slots, GROUP, axis=2)
-    unit_recv = lax.all_to_all(unit_send, "expert", split_axis=2, concat_axis=2, tiled=True)
+    unit_recv = stacked_exchange(unit_send, "expert", 2, 2)
     unit_rows = unit_recv.reshape(stretches, MICRO, slot_count, feature_count)
     top_section = section_index == sections - 1
 

time: 959 us -> 989 us (1.031)
  local copies, waits for them, and re-layouts: 62.3 us -> 82.8 us
    unnamed x13 -> x42, local copies, waits for them, and re-layouts: 1.44 us -> 21.8 us
    dot_general x15, matrix products: 7.67 us -> 27.4 us  [tick_step(): jnp.einsum('rd,hd->rh', grad_rows, down_slab, preferred_element_type=jnp....]
    dot_general x15, matrix products: 17.1 us -> 2.3 us  [tick_step(): jnp.einsum('ect,td->ecd', place_now, grad_in, preferred_element_type=jnp....]
where the time goes in v1:
time: 989 us; the launch traced here: 984 us
  waiting for transfers between devices  516 us (52%)
  starting transfers between devices  160 us (16%)
  matrix products  127 us (13%)
  local copies, waits for them, and re-layouts  82.8 us (8%)
  other arithmetic  53 us (5%)
  blocking collectives  28.9 us (3%)
  between operations  13.9 us (1%)
    all_to_all x15, waiting for transfers between devices, tick_step(): lax.all_to_all(partial_value.reshape(width_all, capacity, feature_count),...  164 us
    all_to_all x15, waiting for transfers between devices, tick_step(): lax.all_to_all(sending, 'expert', split_axis=0, concat_axis=0, tiled=True)  157 us
    ppermute x15, waiting for transfers between devices, shifted(): return lax.ppermute(block, axis, route)  76.5 us
    reduce_scatter x1, waiting for transfers between devices, shards(): lax.psum_scatter(part_up.astype(jnp.bfloat16), 'dp', scatter_dimension=2,...  68 us
    all_to_all x15, starting transfers between devices, tick_step(): lax.all_to_all(sending, 'expert', split_axis=0, concat_axis=0, tiled=True)  67.7 us
    all_to_all x15, starting transfers between devices, tick_step(): lax.all_to_all(partial_value.reshape(width_all, capacity, feature_count),...  62 us
    dot_general x15, matrix products, tick_step(): jnp.einsum('rd,hd->rh', unit_now, gate_slab, preferred_element_type=jnp.f...  40.3 us
    dot_general x15, matrix products, tick_step(): jnp.einsum('rd,hd->rh', unit_now, up_slab, preferred_element_type=jnp.flo...  40.1 us
  transfers between devices with their start and end apart: 51, of which 48 were waited for; matrix products, arithmetic and copies ran while one was open for 3% of the time, Pallas kernels for 0%

profile of v1, /device:TPU:1, one launch (start us, length us, event | category | flops | bytes accessed | tf_op | source)
XLA Modules:
  0.0 983.7 jit_solution(10738537261919837827)
XLA Ops:
  37.1 10.7 %all-to-all-start.2 = ((bf16[32,1,8,1,2,2560]{5,4,2,3,1,0:T(2,128)(2,1)}), bf16[32,1,8,1,2,2560]{5,4,2,3,1,0:T(2,128)(2,1)}, u32[]{:S(2)}, u32[]{:S(2)}) async-start(bf16[32,1,8,1,2,2560]{5,4,2,3,1,0:T(2,128)(2,1)} %fusion.45), calls=%async_computation.2 | async-start | bytes 5242880 | tf_op jit(solution)/shard_map/all_to_all | solution.py:14
  50.1 28.9 %all_gather.12 = bf16[128,2560]{0,1:T(8,128)(2,1)S(1)} all-gather(bf16[128,320]{0,1:T(8,128)(2,1)S(1)} %copy-done.6), channel_id=1, replica_groups=mesh['pipe'=8,'expert'=32,'dp'=2] {'pipe'}, dimensions={1}, use_global_device_ids=true | all-gather | bytes 737280 | tf_op jit(solution)/shard_map/all_gather | solution.py:44
  80.7 26.8 %all-to-all-done.2 = bf16[32,1,8,1,2,2560]{5,4,2,3,1,0:T(2,128)(2,1)} async-done(((bf16[32,1,8,1,2,2560]{5,4,2,3,1,0:T(2,128)(2,1)}), bf16[32,1,8,1,2,2560]{5,4,2,3,1,0:T(2,128)(2,1)}, u32[]{:S(2)}, u32[]{:S(2)}) %all-to-all-start.2) | async-done | bytes 2621472 | tf_op jit(solution)/shard_map/all_to_all | solution.py:14
  123.6 758.2 %while.21 = (s32[]{:T(128)}, bf16[16,2560]{1,0:T(8,128)(2,1)S(1)}, bf16[1,8,64,256]{3,2,1,0:T(8,128)(2,1)}, bf16[1,8,64,256]{3,2,1,0:T(8,128)(2,1)}, s32[]{:T(12...) while((s32[]{:T(128)}, bf16[16,2560]{1,0:T(8,128)(2,1)S(1)}, ...), condition=%wide.region_7.8_spmd, body=%wide.region_3.7_spmd.sunk | while | flops 422298752 | bytes 31978876 | solution.py:140
  132.4 10.5 %all-to-all-done = bf16[32,2,2560]{2,1,0:T(2,128)(2,1)S(1)} async-done(((bf16[32,2,2560]{2,1,0:T(2,128)(2,1)}), bf16[32,2,2560]{2,1,0:T(2,128)(2,1)S(1)}, u32[]{:S(2)}, u32[]{:S(2)}) %all-to-all-start) | async-done | bytes 327712 | tf_op jit(solution)/shard_map/while/body/eval_jaxpr/all_to_all | solution.py:84
  157.8 10.7 %all-to-all-done.1 = bf16[32,2,2560]{2,1,0:T(2,128)(2,1)S(1)} async-done(((bf16[32,2,2560]{2,1,0:T(2,128)(2,1)}), bf16[32,2,2560]{2,1,0:T(2,128)(2,1)S(1)}, u32[]{:S(2)}, u32[]{:S(2)}) %all-to-all-start.1) | async-done | bytes 327712 | tf_op jit(solution)/shard_map/while/body/eval_jaxpr/all_to_all | solution.py:105
  185.7 10.1 %all-to-all-done = bf16[32,2,2560]{2,1,0:T(2,128)(2,1)S(1)} async-done(((bf16[32,2,2560]{2,1,0:T(2,128)(2,1)}), bf16[32,2,2560]{2,1,0:T(2,128)(2,1)S(1)}, u32[]{:S(2)}, u32[]{:S(2)}) %all-to-all-start) | async-done | bytes 327712 | tf_op jit(solution)/shard_map/while/body/eval_jaxpr/all_to_all | solution.py:84
  209.1 10.7 %all-to-all-done.1 = bf16[32,2,2560]{2,1,0:T(2,128)(2,1)S(1)} async-done(((bf16[32,2,2560]{2,1,0:T(2,128)(2,1)}), bf16[32,2,2560]{2,1,0:T(2,128)(2,1)S(1)}, u32[]{:S(2)}, u32[]{:S(2)}) %all-to-all-start.1) | async-done | bytes 327712 | tf_op jit(solution)/shard_map/while/body/eval_jaxpr/all_to_all | solution.py:105
  235.1 10.0 %all-to-all-done = bf16[32,2,2560]{2,1,0:T(2,128)(2,1)S(1)} async-done(((bf16[32,2,2560]{2,1,0:T(2,128)(2,1)}), bf16[32,2,2560]{2,1,0:T(2,128)(2,1)S(1)}, u32[]{:S(2)}, u32[]{:S(2)}) %all-to-all-start) | async-done | bytes 327712 | tf_op jit(solution)/shard_map/while/body/eval_jaxpr/all_to_all | solution.py:84
  258.1 10.6 %all-to-all-done.1 = bf16[32,2,2560]{2,1,0:T(2,128)(2,1)S(1)} async-done(((bf16[32,2,2560]{2,1,0:T(2,128)(2,1)}), bf16[32,2,2560]{2,1,0:T(2,128)(2,1)S(1)}, u32[]{:S(2)}, u32[]{:S(2)}) %all-to-all-start.1) | async-done | bytes 327712 | tf_op jit(solution)/shard_map/while/body/eval_jaxpr/all_to_all | solution.py:105
  306.7 10.6 %all-to-all-done.1 = bf16[32,2,2560]{2,1,0:T(2,128)(2,1)S(1)} async-done(((bf16[32,2,2560]{2,1,0:T(2,128)(2,1)}), bf16[32,2,2560]{2,1,0:T(2,128)(2,1)S(1)}, u32[]{:S(2)}, u32[]{:S(2)}) %all-to-all-start.1) | async-done | bytes 327712 | tf_op jit(solution)/shard_map/while/body/eval_jaxpr/all_to_all | solution.py:105
  333.8 10.0 %all-to-all-done = bf16[32,2,2560]{2,1,0:T(2,128)(2,1)S(1)} async-done(((bf16[32,2,2560]{2,1,0:T(2,128)(2,1)}), bf16[32,2,2560]{2,1,0:T(2,128)(2,1)S(1)}, u32[]{:S(2)}, u32[]{:S(2)}) %all-to-all-start) | async-done | bytes 327712 | tf_op jit(solution)/shard_map/while/body/eval_jaxpr/all_to_all | solution.py:84
  356.8 10.6 %all-to-all-done.1 = bf16[32,2,2560]{2,1,0:T(2,128)(2,1)S(1)} async-done(((bf16[32,2,2560]{2,1,0:T(2,128)(2,1)}), bf16[32,2,2560]{2,1,0:T(2,128)(2,1)S(1)}, u32[]{:S(2)}, u32[]{:S(2)}) %all-to-all-start.1) | async-done | bytes 327712 | tf_op jit(solution)/shard_map/while/body/eval_jaxpr/all_to_all | solution.py:105
  383.3 10.0 %all-to-all-done = bf16[32,2,2560]{2,1,0:T(2,128)(2,1)S(1)} async-done(((bf16[32,2,2560]{2,1,0:T(2,128)(2,1)}), bf16[32,2,2560]{2,1,0:T(2,128)(2,1)S(1)}, u32[]{:S(2)}, u32[]{:S(2)}) %all-to-all-start) | async-done | bytes 327712 | tf_op jit(solution)/shard_map/while/body/eval_jaxpr/all_to_all | solution.py:84
  406.2 10.6 %all-to-all-done.1 = bf16[32,2,2560]{2,1,0:T(2,128)(2,1)S(1)} async-done(((bf16[32,2,2560]{2,1,0:T(2,128)(2,1)}), bf16[32,2,2560]{2,1,0:T(2,128)(2,1)S(1)}, u32[]{:S(2)}, u32[]{:S(2)}) %all-to-all-start.1) | async-done | bytes 327712 | tf_op jit(solution)/shard_map/while/body/eval_jaxpr/all_to_all | solution.py:105
  455.3 12.1 %all-to-all-done.1 = bf16[32,2,2560]{2,1,0:T(2,128)(2,1)S(1)} async-done(((bf16[32,2,2560]{2,1,0:T(2,128)(2,1)}), bf16[32,2,2560]{2,1,0:T(2,128)(2,1)S(1)}, u32[]{:S(2)}, u32[]{:S(2)}) %all-to-all-start.1) | async-done | bytes 327712 | tf_op jit(solution)/shard_map/while/body/eval_jaxpr/all_to_all | solution.py:105
  482.9 11.5 %all-to-all-done = bf16[32,2,2560]{2,1,0:T(2,128)(2,1)S(1)} async-done(((bf16[32,2,2560]{2,1,0:T(2,128)(2,1)}), bf16[32,2,2560]{2,1,0:T(2,128)(2,1)S(1)}, u32[]{:S(2)}, u32[]{:S(2)}) %all-to-all-start) | async-done | bytes 327712 | tf_op jit(solution)/shard_map/while/body/eval_jaxpr/all_to_all | solution.py:84
  507.3 11.1 %all-to-all-done.1 = bf16[32,2,2560]{2,1,0:T(2,128)(2,1)S(1)} async-done(((bf16[32,2,2560]{2,1,0:T(2,128)(2,1)}), bf16[32,2,2560]{2,1,0:T(2,128)(2,1)S(1)}, u32[]{:S(2)}, u32[]{:S(2)}) %all-to-all-start.1) | async-done | bytes 327712 | tf_op jit(solution)/shard_map/while/body/eval_jaxpr/all_to_all | solution.py:105
  536.5 13.3 %all-to-all-done = bf16[32,2,2560]{2,1,0:T(2,128)(2,1)S(1)} async-done(((bf16[32,2,2560]{2,1,0:T(2,128)(2,1)}), bf16[32,2,2560]{2,1,0:T(2,128)(2,1)S(1)}, u32[]{:S(2)}, u32[]{:S(2)}) %all-to-all-start) | async-done | bytes 327712 | tf_op jit(solution)/shard_map/while/body/eval_jaxpr/all_to_all | solution.py:84
  563.3 10.8 %all-to-all-done.1 = bf16[32,2,2560]{2,1,0:T(2,128)(2,1)S(1)} async-done(((bf16[32,2,2560]{2,1,0:T(2,128)(2,1)}), bf16[32,2,2560]{2,1,0:T(2,128)(2,1)S(1)}, u32[]{:S(2)}, u32[]{:S(2)}) %all-to-all-start.1) | async-done | bytes 327712 | tf_op jit(solution)/shard_map/while/body/eval_jaxpr/all_to_all | solution.py:105
  589.1 10.1 %all-to-all-done = bf16[32,2,2560]{2,1,0:T(2,128)(2,1)S(1)} async-done(((bf16[32,2,2560]{2,1,0:T(2,128)(2,1)}), bf16[32,2,2560]{2,1,0:T(2,128)(2,1)S(1)}, u32[]{:S(2)}, u32[]{:S(2)}) %all-to-all-start) | async-done | bytes 327712 | tf_op jit(solution)/shard_map/while/body/eval_jaxpr/all_to_all | solution.py:84
  612.3 10.7 %all-to-all-done.1 = bf16[32,2,2560]{2,1,0:T(2,128)(2,1)S(1)} async-done(((bf16[32,2,2560]{2,1,0:T(2,128)(2,1)}), bf16[32,2,2560]{2,1,0:T(2,128)(2,1)S(1)}, u32[]{:S(2)}, u32[]{:S(2)}) %all-to-all-start.1) | async-done | bytes 327712 | tf_op jit(solution)/shard_map/while/body/eval_jaxpr/all_to_all | solution.py:105
  660.3 10.6 %all-to-all-done.1 = bf16[32,2,2560]{2,1,0:T(2,128)(2,1)S(1)} async-done(((bf16[32,2,2560]{2,1,0:T(2,128)(2,1)}), bf16[32,2,2560]{2,1,0:T(2,128)(2,1)S(1)}, u32[]{:S(2)}, u32[]{:S(2)}) %all-to-all-start.1) | async-done | bytes 327712 | tf_op jit(solution)/shard_map/while/body/eval_jaxpr/all_to_all | solution.py:105
  709.0 10.6 %all-to-all-done.1 = bf16[32,2,2560]{2,1,0:T(2,128)(2,1)S(1)} async-done(((bf16[32,2,2560]{2,1,0:T(2,128)(2,1)}), bf16[32,2,2560]{2,1,0:T(2,128)(2,1)S(1)}, u32[]{:S(2)}, u32[]{:S(2)}) %all-to-all-start.1) | async-done | bytes 327712 | tf_op jit(solution)/shard_map/while/body/eval_jaxpr/all_to_all | solution.py:105
  737.0 10.5 %all-to-all-done = bf16[32,2,2560]{2,1,0:T(2,128)(2,1)S(1)} async-done(((bf16[32,2,2560]{2,1,0:T(2,128)(2,1)}), bf16[32,2,2560]{2,1,0:T(2,128)(2,1)S(1)}, u32[]{:S(2)}, u32[]{:S(2)}) %all-to-all-start) | async-done | bytes 327712 | tf_op jit(solution)/shard_map/while/body/eval_jaxpr/all_to_all | solution.py:84
  760.3 11.1 %all-to-all-done.1 = bf16[32,2,2560]{2,1,0:T(2,128)(2,1)S(1)} async-done(((bf16[32,2,2560]{2,1,0:T(2,128)(2,1)}), bf16[32,2,2560]{2,1,0:T(2,128)(2,1)S(1)}, u32[]{:S(2)}, u32[]{:S(2)}) %all-to-all-start.1) | async-done | bytes 327712 | tf_op jit(solution)/shard_map/while/body/eval_jaxpr/all_to_all | solution.py:105
  787.3 10.5 %all-to-all-done = bf16[32,2,2560]{2,1,0:T(2,128)(2,1)S(1)} async-done(((bf16[32,2,2560]{2,1,0:T(2,128)(2,1)}), bf16[32,2,2560]{2,1,0:T(2,128)(2,1)S(1)}, u32[]{:S(2)}, u32[]{:S(2)}) %all-to-all-start) | async-done | bytes 327712 | tf_op jit(solution)/shard_map/while/body/eval_jaxpr/all_to_all | solution.py:84
  810.6 11.1 %all-to-all-done.1 = bf16[32,2,2560]{2,1,0:T(2,128)(2,1)S(1)} async-done(((bf16[32,2,2560]{2,1,0:T(2,128)(2,1)}), bf16[32,2,2560]{2,1,0:T(2,128)(2,1)S(1)}, u32[]{:S(2)}, u32[]{:S(2)}) %all-to-all-start.1) | async-done | bytes 327712 | tf_op jit(solution)/shard_map/while/body/eval_jaxpr/all_to_all | solution.py:105
  836.4 10.4 %all-to-all-done = bf16[32,2,2560]{2,1,0:T(2,128)(2,1)S(1)} async-done(((bf16[32,2,2560]{2,1,0:T(2,128)(2,1)}), bf16[32,2,2560]{2,1,0:T(2,128)(2,1)S(1)}, u32[]{:S(2)}, u32[]{:S(2)}) %all-to-all-start) | async-done | bytes 327712 | tf_op jit(solution)/shard_map/while/body/eval_jaxpr/all_to_all | solution.py:84
  859.7 12.3 %all-to-all-done.1 = bf16[32,2,2560]{2,1,0:T(2,128)(2,1)S(1)} async-done(((bf16[32,2,2560]{2,1,0:T(2,128)(2,1)}), bf16[32,2,2560]{2,1,0:T(2,128)(2,1)S(1)}, u32[]{:S(2)}, u32[]{:S(2)}) %all-to-all-start.1) | async-done | bytes 327712 | tf_op jit(solution)/shard_map/while/body/eval_jaxpr/all_to_all | solution.py:105
  887.7 68.0 %reduce-scatter.5.cloned.1.call-done = bf16[1,256,1280]{2,1,0:T(8,128)(2,1)} async-done(((bf16[1,256,2560]{2,1,0:T(8,128)(2,1)}), bf16[1,256,1280]{2,1,0:T(8,128)(2,1)}) %reduce-scatter.5.cloned.1.call-update) | async-done | bytes 655376 | tf_op jit(solution)/shard_map/reduce_scatter | solution.py:158
  955.8 21.4 %reduce-scatter.3.cloned.1.call-done = bf16[1,256,1280]{2,1,0:T(8,128)(2,1)} async-done(((bf16[1,256,2560]{2,1,0:T(8,128)(2,1)}), bf16[1,256,1280]{2,1,0:T(8,128)(2,1)}) %reduce-scatter.3.cloned.1.call-update) | async-done | bytes 655376 | tf_op jit(solution)/shard_map/reduce_scatter | solution.py:155
  (599 shorter events, 530.7 us)
Async XLA Ops:
  37.1 70.4 %all-to-all-start.2 = ((bf16[32,1,8,1,2,2560]{5,4,2,3,1,0:T(2,128)(2,1)}), bf16[32,1,8,1,2,2560]{5,4,2,3,1,0:T(2,128)(2,1)}, u32[]{:S(2)}, u32[]{:S(2)}) async-start(bf16[32,1,8,1,2,2560]{5,4,2,3,1,0:T(2,128)(2,1)} %fusion.45), calls=%async_computation.2 | async-start | bytes 5242880 | tf_op jit(solution)/shard_map/all_to_all | solution.py:14
  47.9 74.3 %all-gather.4.cloned.1.call-start = ((), (), s32[]{:S(2)}) async-start(), calls=%async_computation.5 | async-start | bytes 1966080 | tf_op jit(solution)/shard_map/all_gather | solution.py:49
  48.6 73.6 %all-gather.6.cloned.1.call-start = ((), (), s32[]{:S(2)}) async-start(), calls=%async_computation.6 | async-start | bytes 1966080 | tf_op jit(solution)/shard_map/all_gather | solution.py:48
  49.4 72.8 %all-gather.8.cloned.1.call-start = ((), (), s32[]{:S(2)}) async-start(), calls=%async_computation.7 | async-start | bytes 1966080 | tf_op jit(solution)/shard_map/all_gather | solution.py:47
  50.1 905.7 %reduce-scatter.5.cloned.1.call-start = ((), (), s32[]{:S(2)}) async-start(), calls=%async_computation.9 | async-start | bytes 1966080 | tf_op jit(solution)/shard_map/reduce_scatter | solution.py:158
  124.9 18.0 %all-to-all-start = ((bf16[32,2,2560]{2,1,0:T(2,128)(2,1)}), bf16[32,2,2560]{2,1,0:T(2,128)(2,1)S(1)}, u32[]{:S(2)}, u32[]{:S(2)}) async-start(bf16[32,2,2560]{2,1,0:T(2,128)(2,1)} %bitcast.270), calls=%async_computation | async-start | bytes 655360 | tf_op jit(solution)/shard_map/while/body/eval_jaxpr/all_to_all | solution.py:84
  151.8 16.7 %all-to-all-start.1 = ((bf16[32,2,2560]{2,1,0:T(2,128)(2,1)}), bf16[32,2,2560]{2,1,0:T(2,128)(2,1)S(1)}, u32[]{:S(2)}, u32[]{:S(2)}) async-start(bf16[32,2,2560]{2,1,0:T(2,128)(2,1)} %reshape.458), calls=%async_computation.1 | async-start | bytes 655360 | tf_op jit(solution)/shard_map/while/body/eval_jaxpr/all_to_all | solution.py:105
  178.6 17.2 %all-to-all-start = ((bf16[32,2,2560]{2,1,0:T(2,128)(2,1)}), bf16[32,2,2560]{2,1,0:T(2,128)(2,1)S(1)}, u32[]{:S(2)}, u32[]{:S(2)}) async-start(bf16[32,2,2560]{2,1,0:T(2,128)(2,1)} %bitcast.270), calls=%async_computation | async-start | bytes 655360 | tf_op jit(solution)/shard_map/while/body/eval_jaxpr/all_to_all | solution.py:84
  204.8 15.1 %all-to-all-start.1 = ((bf16[32,2,2560]{2,1,0:T(2,128)(2,1)}), bf16[32,2,2560]{2,1,0:T(2,128)(2,1)S(1)}, u32[]{:S(2)}, u32[]{:S(2)}) async-start(bf16[32,2,2560]{2,1,0:T(2,128)(2,1)} %reshape.458), calls=%async_computation.1 | async-start | bytes 655360 | tf_op jit(solution)/shard_map/while/body/eval_jaxpr/all_to_all | solution.py:105
  230.1 15.1 %all-to-all-start = ((bf16[32,2,2560]{2,1,0:T(2,128)(2,1)}), bf16[32,2,2560]{2,1,0:T(2,128)(2,1)S(1)}, u32[]{:S(2)}, u32[]{:S(2)}) async-start(bf16[32,2,2560]{2,1,0:T(2,128)(2,1)} %bitcast.270), calls=%async_computation | async-start | bytes 655360 | tf_op jit(solution)/shard_map/while/body/eval_jaxpr/all_to_all | solution.py:84
  254.0 14.7 %all-to-all-start.1 = ((bf16[32,2,2560]{2,1,0:T(2,128)(2,1)}), bf16[32,2,2560]{2,1,0:T(2,128)(2,1)S(1)}, u32[]{:S(2)}, u32[]{:S(2)}) async-start(bf16[32,2,2560]{2,1,0:T(2,128)(2,1)} %reshape.458), calls=%async_computation.1 | async-start | bytes 655360 | tf_op jit(solution)/shard_map/while/body/eval_jaxpr/all_to_all | solution.py:105
  279.0 14.8 %all-to-all-start = ((bf16[32,2,2560]{2,1,0:T(2,128)(2,1)}), bf16[32,2,2560]{2,1,0:T(2,128)(2,1)S(1)}, u32[]{:S(2)}, u32[]{:S(2)}) async-start(bf16[32,2,2560]{2,1,0:T(2,128)(2,1)} %bitcast.270), calls=%async_computation | async-start | bytes 655360 | tf_op jit(solution)/shard_map/while/body/eval_jaxpr/all_to_all | solution.py:84
  302.7 14.7 %all-to-all-start.1 = ((bf16[32,2,2560]{2,1,0:T(2,128)(2,1)}), bf16[32,2,2560]{2,1,0:T(2,128)(2,1)S(1)}, u32[]{:S(2)}, u32[]{:S(2)}) async-start(bf16[32,2,2560]{2,1,0:T(2,128)(2,1)} %reshape.458), calls=%async_computation.1 | async-start | bytes 655360 | tf_op jit(solution)/shard_map/while/body/eval_jaxpr/all_to_all | solution.py:105
  329.0 14.8 %all-to-all-start = ((bf16[32,2,2560]{2,1,0:T(2,128)(2,1)}), bf16[32,2,2560]{2,1,0:T(2,128)(2,1)S(1)}, u32[]{:S(2)}, u32[]{:S(2)}) async-start(bf16[32,2,2560]{2,1,0:T(2,128)(2,1)} %bitcast.270), calls=%async_computation | async-start | bytes 655360 | tf_op jit(solution)/shard_map/while/body/eval_jaxpr/all_to_all | solution.py:84
  378.5 14.8 %all-to-all-start = ((bf16[32,2,2560]{2,1,0:T(2,128)(2,1)}), bf16[32,2,2560]{2,1,0:T(2,128)(2,1)S(1)}, u32[]{:S(2)}, u32[]{:S(2)}) async-start(bf16[32,2,2560]{2,1,0:T(2,128)(2,1)} %bitcast.270), calls=%async_computation | async-start | bytes 655360 | tf_op jit(solution)/shard_map/while/body/eval_jaxpr/all_to_all | solution.py:84
  427.6 14.8 %all-to-all-start = ((bf16[32,2,2560]{2,1,0:T(2,128)(2,1)}), bf16[32,2,2560]{2,1,0:T(2,128)(2,1)S(1)}, u32[]{:S(2)}, u32[]{:S(2)}) async-start(bf16[32,2,2560]{2,1,0:T(2,128)(2,1)} %bitcast.270), calls=%async_computation | async-start | bytes 655360 | tf_op jit(solution)/shard_map/while/body/eval_jaxpr/all_to_all | solution.py:84
  451.3 16.1 %all-to-all-start.1 = ((bf16[32,2,2560]{2,1,0:T(2,128)(2,1)}), bf16[32,2,2560]{2,1,0:T(2,128)(2,1)S(1)}, u32[]{:S(2)}, u32[]{:S(2)}) async-start(bf16[32,2,2560]{2,1,0:T(2,128)(2,1)} %reshape.458), calls=%async_computation.1 | async-start | bytes 655360 | tf_op jit(solution)/shard_map/while/body/eval_jaxpr/all_to_all | solution.py:105
  478.2 16.3 %all-to-all-start = ((bf16[32,2,2560]{2,1,0:T(2,128)(2,1)}), bf16[32,2,2560]{2,1,0:T(2,128)(2,1)S(1)}, u32[]{:S(2)}, u32[]{:S(2)}) async-start(bf16[32,2,2560]{2,1,0:T(2,128)(2,1)} %bitcast.270), calls=%async_computation | async-start | bytes 655360 | tf_op jit(solution)/shard_map/while/body/eval_jaxpr/all_to_all | solution.py:84
  503.4 15.1 %all-to-all-start.1 = ((bf16[32,2,2560]{2,1,0:T(2,128)(2,1)}), bf16[32,2,2560]{2,1,0:T(2,128)(2,1)S(1)}, u32[]{:S(2)}, u32[]{:S(2)}) async-start(bf16[32,2,2560]{2,1,0:T(2,128)(2,1)} %reshape.458), calls=%async_computation.1 | async-start | bytes 655360 | tf_op jit(solution)/shard_map/while/body/eval_jaxpr/all_to_all | solution.py:105
  530.9 18.9 %all-to-all-start = ((bf16[32,2,2560]{2,1,0:T(2,128)(2,1)}), bf16[32,2,2560]{2,1,0:T(2,128)(2,1)S(1)}, u32[]{:S(2)}, u32[]{:S(2)}) async-start(bf16[32,2,2560]{2,1,0:T(2,128)(2,1)} %bitcast.270), calls=%async_computation | async-start | bytes 655360 | tf_op jit(solution)/shard_map/while/body/eval_jaxpr/all_to_all | solution.py:84
  558.7 15.4 %all-to-all-start.1 = ((bf16[32,2,2560]{2,1,0:T(2,128)(2,1)}), bf16[32,2,2560]{2,1,0:T(2,128)(2,1)S(1)}, u32[]{:S(2)}, u32[]{:S(2)}) async-start(bf16[32,2,2560]{2,1,0:T(2,128)(2,1)} %reshape.458), calls=%async_computation.1 | async-start | bytes 655360 | tf_op jit(solution)/shard_map/while/body/eval_jaxpr/all_to_all | solution.py:105
  583.6 15.5 %all-to-all-start = ((bf16[32,2,2560]{2,1,0:T(2,128)(2,1)}), bf16[32,2,2560]{2,1,0:T(2,128)(2,1)S(1)}, u32[]{:S(2)}, u32[]{:S(2)}) async-start(bf16[32,2,2560]{2,1,0:T(2,128)(2,1)} %bitcast.270), calls=%async_computation | async-start | bytes 655360 | tf_op jit(solution)/shard_map/while/body/eval_jaxpr/all_to_all | solution.py:84
  608.1 14.9 %all-to-all-start.1 = ((bf16[32,2,2560]{2,1,0:T(2,128)(2,1)}), bf16[32,2,2560]{2,1,0:T(2,128)(2,1)S(1)}, u32[]{:S(2)}, u32[]{:S(2)}) async-start(bf16[32,2,2560]{2,1,0:T(2,128)(2,1)} %reshape.458), calls=%async_computation.1 | async-start | bytes 655360 | tf_op jit(solution)/shard_map/while/body/eval_jaxpr/all_to_all | solution.py:105
  632.5 14.8 %all-to-all-start = ((bf16[32,2,2560]{2,1,0:T(2,128)(2,1)}), bf16[32,2,2560]{2,1,0:T(2,128)(2,1)S(1)}, u32[]{:S(2)}, u32[]{:S(2)}) async-start(bf16[32,2,2560]{2,1,0:T(2,128)(2,1)} %bitcast.270), calls=%async_computation | async-start | bytes 655360 | tf_op jit(solution)/shard_map/while/body/eval_jaxpr/all_to_all | solution.py:84
  681.3 14.8 %all-to-all-start = ((bf16[32,2,2560]{2,1,0:T(2,128)(2,1)}), bf16[32,2,2560]{2,1,0:T(2,128)(2,1)S(1)}, u32[]{:S(2)}, u32[]{:S(2)}) async-start(bf16[32,2,2560]{2,1,0:T(2,128)(2,1)} %bitcast.270), calls=%async_computation | async-start | bytes 655360 | tf_op jit(solution)/shard_map/while/body/eval_jaxpr/all_to_all | solution.py:84
  732.3 15.2 %all-to-all-start = ((bf16[32,2,2560]{2,1,0:T(2,128)(2,1)}), bf16[32,2,2560]{2,1,0:T(2,128)(2,1)S(1)}, u32[]{:S(2)}, u32[]{:S(2)}) async-start(bf16[32,2,2560]{2,1,0:T(2,128)(2,1)} %bitcast.270), calls=%async_computation | async-start | bytes 655360 | tf_op jit(solution)/shard_map/while/body/eval_jaxpr/all_to_all | solution.py:84
  756.4 15.1 %all-to-all-start.1 = ((bf16[32,2,2560]{2,1,0:T(2,128)(2,1)}), bf16[32,2,2560]{2,1,0:T(2,128)(2,1)S(1)}, u32[]{:S(2)}, u32[]{:S(2)}) async-start(bf16[32,2,2560]{2,1,0:T(2,128)(2,1)} %reshape.458), calls=%async_computation.1 | async-start | bytes 655360 | tf_op jit(solution)/shard_map/while/body/eval_jaxpr/all_to_all | solution.py:105
  782.5 15.2 %all-to-all-start = ((bf16[32,2,2560]{2,1,0:T(2,128)(2,1)}), bf16[32,2,2560]{2,1,0:T(2,128)(2,1)S(1)}, u32[]{:S(2)}, u32[]{:S(2)}) async-start(bf16[32,2,2560]{2,1,0:T(2,128)(2,1)} %bitcast.270), calls=%async_computation | async-start | bytes 655360 | tf_op jit(solution)/shard_map/while/body/eval_jaxpr/all_to_all | solution.py:84
  806.6 15.1 %all-to-all-start.1 = ((bf16[32,2,2560]{2,1,0:T(2,128)(2,1)}), bf16[32,2,2560]{2,1,0:T(2,128)(2,1)S(1)}, u32[]{:S(2)}, u32[]{:S(2)}) async-start(bf16[32,2,2560]{2,1,0:T(2,128)(2,1)} %reshape.458), calls=%async_computation.1 | async-start | bytes 655360 | tf_op jit(solution)/shard_map/while/body/eval_jaxpr/all_to_all | solution.py:105
  831.7 15.2 %all-to-all-start = ((bf16[32,2,2560]{2,1,0:T(2,128)(2,1)}), bf16[32,2,2560]{2,1,0:T(2,128)(2,1)S(1)}, u32[]{:S(2)}, u32[]{:S(2)}) async-start(bf16[32,2,2560]{2,1,0:T(2,128)(2,1)} %bitcast.270), calls=%async_computation | async-start | bytes 655360 | tf_op jit(solution)/shard_map/while/body/eval_jaxpr/all_to_all | solution.py:84
  855.7 16.2 %all-to-all-start.1 = ((bf16[32,2,2560]{2,1,0:T(2,128)(2,1)}), bf16[32,2,2560]{2,1,0:T(2,128)(2,1)S(1)}, u32[]{:S(2)}, u32[]{:S(2)}) async-start(bf16[32,2,2560]{2,1,0:T(2,128)(2,1)} %reshape.458), calls=%async_computation.1 | async-start | bytes 655360 | tf_op jit(solution)/shard_map/while/body/eval_jaxpr/all_to_all | solution.py:105
  885.7 91.4 %reduce-scatter.3.cloned.1.call-start = ((), (), s32[]{:S(2)}) async-start(), calls=%async_computation.8 | async-start | bytes 1966080 | tf_op jit(solution)/shard_map/reduce_scatter | solution.py:155
  (84 other events, 1079.2 us)
Sparse Core Ops, SparseCore 0:
  50.8 23.6 all-gather.3
  76.6 18.8 all-gather.5
  97.6 18.8 all-gather.7
  885.8 69.8 reduce-scatter.4
  959.0 18.1 reduce-scatter.2
